TPU v7x, 128 devices: a whole 4x4x4 slice. The times are simulated.
128 devices in a mesh: base: 16 (over z, y), freq: 8 (over x, core).
Axes of the slice: x: 4, y: 4, z: 4, core: 2. Of those that a mesh axis runs over, the one named last changes fastest.
Arguments:
- visibilities: bfloat16 [2, 16384, 2048], P(None, 'base', 'freq'), may hold values from -0.01171875 to 0.01171875
- anchor: bfloat16 [2, 16384], P(None, 'base'), may hold values from 4 to 60, as said below
- drift: bfloat16 [2, 16384], P(None, 'base'), may hold values from -0.01953125 to 0.01953125
- target: int32 [16384, 1], P('base'), may hold values from 0 to 127; in each aligned block of 1024 rows (0 to 1023, 1024 to 2047, ...) at most 8 rows name the same one
- subgrid_w: float32 [128], P('base'), may hold values from -1 to 1
- facet_owner: int32 [128, 1], P('base'), may hold values from 0 to 15; in each aligned block of 8 rows (0 to 7, 8 to 15, ...) at most 2 rows name the same one
- row_offset: int32 [128], P('base'), may hold values from 0 to 64
- col_offset: int32 [128], P('base'), may hold values from 0 to 16320
Outputs:
- grid: float32 [2, 2048, 16384], P(None, 'base')
Inputs may be any that keep to these rules, and one draw needn't show every extreme that they name: `target`: among the 1024 blocks of one index of base no subgrid is named more than 8 times. `facet_owner`: among the 8 subgrids of one index of base no owner is named more than 2 times. anchor[k,b] + 2048 drift[k,b] lies between 4 and 60, up to the rounding of drift.
All inputs are finite; a program needn't handle non-finite values.
Results may differ from a plain program's by a relative error of at most 0.0038.
Values may be sent and summed in bfloat16 or wider, within the bound.
A program may use at most 128 MiB of HBM per device.

v0:
```python
import math
import jax
import jax.numpy as jnp
from jax import lax
from jax.sharding import PartitionSpec as P

G = 64
GY = 16384
CAP = 8
FCAP = 2
FR = 128


def slot_table(target, groups, depth):
    total = target.shape[0]
    hits = (target[:, None] == jnp.arange(groups, dtype=jnp.int32)[None, :]).astype(jnp.int32)
    before = jnp.cumsum(hits, axis=0) - hits
    ranking = jnp.sum(before * hits, axis=1)
    placed = target * depth + ranking
    match = placed[None, :] == jnp.arange(groups * depth, dtype=jnp.int32)[:, None]
    source = jnp.sum(jnp.where(match, jnp.arange(total, dtype=jnp.int32)[None, :], 0), axis=1)
    filled = jnp.any(match, axis=1)
    return (source, filled)


def phase_table(start, slope, first, channels):
    pixels = (jnp.arange(G, dtype=jnp.int32) - G // 2).astype(jnp.float32) * (2.0 * math.pi / G)
    angles = jnp.concatenate([pixels, pixels])
    shifts = jnp.concatenate(
        [jnp.zeros((G,), jnp.float32), jnp.full((G,), -0.5 * math.pi, jnp.float32)]
    )
    coarse = (first + 16 * jnp.arange(channels // 16, dtype=jnp.int32)).astype(jnp.float32)
    fine = jnp.arange(16, dtype=jnp.int32).astype(jnp.float32)
    centre = start[:, None] + coarse[None, :] * slope[:, None] - 0.5 * G
    outer = centre[:, :, None] * angles + shifts
    inner = (fine[None, :] * slope[:, None])[:, :, None] * angles
    table = (
        jnp.cos(outer)[:, :, None, :] * jnp.cos(inner)[:, None, :, :]
        - jnp.sin(outer)[:, :, None, :] * jnp.sin(inner)[:, None, :, :]
    )
    return table.reshape(start.shape[0], channels, 2 * G)


def grid_one(data, where, first):
    bound = data.shape[1]
    channels = data.shape[2]
    values = where.astype(jnp.float32)
    left = (
        phase_table(values[0], values[2], first, channels)
        .astype(jnp.bfloat16)
        .reshape(bound * channels, 2 * G)
    )
    right = phase_table(values[1], values[3], first, channels)
    signs = jnp.concatenate([-jnp.ones((G,), jnp.float32), jnp.ones((G,), jnp.float32)])
    swapped = jnp.roll(right, G, axis=2) * signs
    real_part = data[0].astype(jnp.float32)[:, :, None]
    imag_part = data[1].astype(jnp.float32)[:, :, None]
    weighted = (
        (real_part * right + imag_part * swapped)
        .astype(jnp.bfloat16)
        .reshape(bound * channels, 2 * G)
    )
    product = lax.dot_general(
        left, weighted, (((0,), (0,)), ((), ())), preferred_element_type=jnp.float32
    )
    return jnp.stack([product[:G, :G] - product[G:, G:], product[:G, G:] + product[G:, :G]])


def to_patch(image, weight):
    axis_values = (jnp.arange(G, dtype=jnp.int32) - G // 2).astype(jnp.float32) / (0.5 * G)
    radius = axis_values[:, None] ** 2 + axis_values[None, :] ** 2
    phase = math.pi * weight[:, None, None] * radius
    cosine, sine = (jnp.cos(phase), jnp.sin(phase))
    kernel_real = image[:, 0] * cosine - image[:, 1] * sine
    kernel_imag = image[:, 0] * sine + image[:, 1] * cosine
    index = jnp.arange(G, dtype=jnp.int32)
    turns = (index[:, None] * index[None, :] % G).astype(jnp.float32) * (2.0 * math.pi / G)
    table_real, table_imag = (jnp.cos(turns), -jnp.sin(turns))
    highest = lax.Precision.HIGHEST

    def from_left(matrix, field):
        return jnp.einsum("jl,slm->sjm", matrix, field, precision=highest)

    def from_right(field, matrix):
        return jnp.einsum("sjm,km->sjk", field, matrix, precision=highest)

    turned_real = from_left(table_real, kernel_real) - from_left(table_imag, kernel_imag)
    turned_imag = from_left(table_real, kernel_imag) + from_left(table_imag, kernel_real)
    patch_real = from_right(turned_real, table_real) - from_right(turned_imag, table_imag)
    patch_imag = from_right(turned_real, table_imag) + from_right(turned_imag, table_real)
    return jnp.stack([patch_real, patch_imag], axis=1) * (1.0 / G)


def per_device(visibilities, anchor, drift, target, subgrid_w, facet_owner, row_offset, col_offset):
    base_count = lax.axis_size("base")
    own_subgrids = subgrid_w.shape[0]
    all_subgrids = own_subgrids * base_count
    channels = visibilities.shape[2]
    first = lax.axis_index("freq") * channels
    source, filled = slot_table(target[:, 0], all_subgrids, CAP)
    picked = jnp.where(
        filled[None, :, None], jnp.take(visibilities, source, axis=1), jnp.zeros((), jnp.bfloat16)
    )
    slotted = picked.reshape(2, all_subgrids, CAP, channels)
    places = jnp.concatenate([anchor, drift], axis=0)
    located = jnp.where(
        filled[None, :], jnp.take(places, source, axis=1), jnp.zeros((), jnp.bfloat16)
    )
    located = located.reshape(4, all_subgrids, CAP)
    grid_data = jnp.moveaxis(slotted, 1, 0)
    grid_where = jnp.moveaxis(located, 1, 0)

    def single(item):
        return grid_one(item[0], item[1], first)

    images = lax.psum_scatter(
        lax.map(single, (grid_data, grid_where)), "base", scatter_dimension=0, tiled=True
    )
    images = lax.psum(images, "freq")
    patches = to_patch(images, subgrid_w)
    chosen, kept = slot_table(facet_owner[:, 0], base_count, FCAP)
    flattened = patches.reshape(own_subgrids, 2 * G * G)
    outgoing = jnp.where(kept[:, None], jnp.take(flattened, chosen, axis=0), 0.0)
    spots = jnp.stack([row_offset, col_offset], axis=1).astype(jnp.float32)
    sent_spots = jnp.where(kept[:, None], jnp.take(spots, chosen, axis=0), 0.0)
    arrived, arrived_spots = (
        lax.all_to_all(outgoing, "base", split_axis=0, concat_axis=0, tiled=True),
        lax.all_to_all(sent_spots, "base", split_axis=0, concat_axis=0, tiled=True),
    )
    corners = arrived_spots.astype(jnp.int32)

    def deposit(position, facet):
        start = (jnp.zeros((), jnp.int32), corners[position, 0], corners[position, 1])
        region = lax.dynamic_slice(facet, start, (2, G, G))
        patch = arrived[position].reshape(2, G, G)
        return lax.dynamic_update_slice(facet, region + patch, start)

    return lax.fori_loop(0, arrived.shape[0], deposit, jnp.zeros((2, FR, GY), jnp.float32))


def solution(mesh):
    return jax.shard_map(
        per_device,
        mesh=mesh,
        in_specs=(
            P(None, "base", "freq"),
            P(None, "base"),
            P(None, "base"),
            P("base", None),
            P("base"),
            P("base", None),
            P("base"),
            P("base"),
        ),
        out_specs=P(None, "base", None),
        check_vma=False,
    )
```

profile of v0, /device:TPU:23, one launch (start us, length us, event | category | flops | bytes accessed | tf_op | source)
XLA Modules:
  0.0 998.7 jit_solution(2251787866545427747)
XLA Ops:
  15.9 5.3 gather_fusion.2
  21.9 490.5 %while.26 = (s32[]{:T(128)}, f32[128,2,64,64]{3,2,1,0:T(8,128)}, bf16[128,4,8]{2,1,0:T(4,128)(2,1)S(1)}, s32[]{:T(128)}, bf16[128,2,8,256]{3,2,0,1:T(8,128)(2,1)...) while((s32[]{:T(128)}, f32[128,2,64,64]{3,2,1,0:T(8,128)}, bf16[128,4,8]{2,1,0:T(4,128)(2,1)S(1)}, ...), condition=%wide.region_10.11_spmd, body=%wide.region_9.10_spmd.sunk | while | flops 71423392 | bytes 5864877 | solution.py:117
  515.2 7.7 all-to-all-start
  523.2 74.6 %reduce-scatter.2.cloned.1.call-done = f32[8,2,64,64]{3,2,1,0:T(8,128)} async-done(((f32[128,2,64,64]{3,2,1,0:T(8,128)}), f32[8,2,64,64]{3,2,1,0:T(8,128)}) %reduce-scatter.2.cloned.1.call-update) | async-done | bytes 262160 | tf_op jit(solution)/shard_map/reduce_scatter | solution.py:116
  597.8 62.8 %all-reduce.2.cloned.1.call-done = f32[8,2,64,64]{3,2,1,0:T(8,128)} async-done(((f32[8,2,64,64]{3,2,1,0:T(8,128)}), f32[8,2,64,64]{3,2,1,0:T(8,128)}) %all-reduce.2.cloned.1.call-update) | async-done | bytes 262160 | tf_op jit(solution)/shard_map/psum | solution.py:119
  677.5 6.9 all-to-all-start.1
  684.6 15.4 %all-to-all-done.1 = f32[16,2,8192]{2,1,0:T(2,128)S(1)} async-done(((f32[16,2,8192]{2,1,0:T(2,128)}), f32[16,2,8192]{2,1,0:T(2,128)S(1)}, u32[]{:S(2)}, u32[]{:S(2)}) %all-to-all-start.1) | async-done | bytes 1048608 | tf_op jit(solution)/shard_map/all_to_all | solution.py:127
  700.8 8.1 broadcast_in_dim.170
  708.9 283.0 %while.27 = (s32[]{:T(128)}, f32[2,128,16384]{2,1,0:T(8,128)}, s32[32,2]{0,1:T(2,128)S(1)}, f32[32,8192]{1,0:T(8,128)S(1)}, s32[]{:T(128)}, /*index=5*/s32[]{:T(128)}, s32[]{:T(128)}, s32[]{:T(128)}) while((s32[]{:T(128)}, f32[2,128,16384]{2,1,0:T(8,128)}, s32[32,2]{0,1:T(2,128)S(1)}, f32[32,8192]{1,0:T(8,128)S(1)}, s32[]{:T(128)}, ...), condition=%wide.region_14.15_spmd, body=%wide.region_13.14_spmd.sunk | while | flops 8200 | bytes 295109 | solution.py:138
  714.5 3.4 dynamic_update_slice.19
  723.4 3.4 dynamic_update_slice.19
  732.4 3.4 dynamic_update_slice.19
  759.1 3.3 dynamic_update_slice.19
  776.9 3.3 dynamic_update_slice.19
  785.8 3.3 dynamic_update_slice.19
  811.8 3.3 dynamic_update_slice.19
  846.2 3.4 dynamic_update_slice.19
  855.1 3.3 dynamic_update_slice.19
  864.1 3.3 dynamic_update_slice.19
  908.6 3.3 dynamic_update_slice.19
  926.4 3.3 dynamic_update_slice.19
  944.1 3.4 dynamic_update_slice.19
  961.9 3.4 dynamic_update_slice.19
  979.8 3.3 dynamic_update_slice.19
  (2275 shorter events, 625.6 us)
Async XLA Ops:
  6.5 9.4 copy-start
  6.5 15.3 %copy-start.6 = (f32[128]{0:T(128)S(1)}, f32[128]{0:T(128)}, u32[]{:S(2)}) copy-start(f32[128]{0:T(128)} %constant.174.clone.1) | copy-start | bytes 1540
  6.5 15.3 %copy-start.1 = (f32[128]{0:T(128)S(1)}, f32[128]{0:T(128)}, u32[]{:S(2)}) copy-start(f32[128]{0:T(128)} %constant.173.clone.1) | copy-start | bytes 1540
  6.5 591.3 %reduce-scatter.2.cloned.1.call-start = ((), (), s32[]{:S(2)}) async-start(), calls=%async_computation.3 | async-start | bytes 8912896 | tf_op jit(solution)/shard_map/reduce_scatter | solution.py:116
  512.3 0.7 copy-start.3
  512.3 0.7 copy-start.4
  512.3 0.8 copy-start.2
  512.3 85.5 %copy-start.5 = (f32[8]{0:T(128)S(1)}, f32[8]{0:T(128)}, u32[]{:S(2)}) copy-start(f32[8]{0:T(128)} %param.16) | copy-start | bytes 100
  515.2 162.3 %all-to-all-start = ((f32[16,2,2]{1,2,0:T(2,128)}), f32[16,2,2]{1,2,0:T(2,128)S(1)}, u32[]{:S(2)}, u32[]{:S(2)}) async-start(f32[16,2,2]{1,2,0:T(2,128)} %copy.84), calls=%async_computation | async-start | bytes 32768 | tf_op jit(solution)/shard_map/all_to_all | solution.py:128
  522.9 137.7 %all-reduce.2.cloned.1.call-start = ((), (), s32[]{:S(2)}) async-start(), calls=%async_computation.4 | async-start | bytes 1048576 | tf_op jit(solution)/shard_map/psum | solution.py:119
  677.5 22.5 %all-to-all-start.1 = ((f32[16,2,8192]{2,1,0:T(2,128)}), f32[16,2,8192]{2,1,0:T(2,128)S(1)}, u32[]{:S(2)}, u32[]{:S(2)}) async-start(f32[16,2,8192]{2,1,0:T(2,128)} %select_select_fusion), calls=%async_computation.2 | async-start | bytes 2097152 | tf_op jit(solution)/shard_map/all_to_all | solution.py:127
Sparse Core Ops, SparseCore 0:
  512.5 85.2 reduce-scatter.1
  600.1 60.4 all-reduce.1
where the time goes:
time: 1010 us; the launch traced here: 999 us
  other arithmetic  298 us (30%)
  local copies, waits for them, and re-layouts  220 us (22%)
  matrix products  171 us (17%)
  waiting for transfers between devices  153 us (15%)
  loops' own time  129 us (13%)
  starting transfers between devices  14.8 us (1%)
  between operations  13.7 us (1%)
    dot_general x128, matrix products, grid_one(): lax.dot_general(left, weighted, (((0,), (0,)), ((), ())), preferred_eleme...  158 us
    cos x128, other arithmetic, phase_table(): jnp.cos(outer)[:, :, None, :] * jnp.cos(inner)[:, None, :, :]  126 us
    another operation x1, loops' own time, per_device(): lax.fori_loop(0, arrived.shape[0], deposit, jnp.zeros((2, FR, GY), jnp.fl...  121 us
    dynamic_update_slice x32, local copies, waits for them, and re-layouts, deposit(): return lax.dynamic_update_slice(facet, region + patch, start)  104 us
    dynamic_update_slice x128, other arithmetic, per_device(): lax.map(single, (grid_data, grid_where))  82.3 us
    reduce_scatter x1, waiting for transfers between devices, per_device(): lax.psum_scatter(lax.map(single, (grid_data, grid_where)), 'base', scatte...  74.6 us
    psum x1, waiting for transfers between devices, per_device(): images = lax.psum(images, 'freq')  62.8 us
    slice x128, local copies, waits for them, and re-layouts, grid_one(): swapped = jnp.roll(right, G, axis=2) * signs  44.2 us
  transfers between devices with their start and end apart: 4, of which 3 were waited for; matrix products, arithmetic and copies ran while one was open for 2% of the time, Pallas kernels for 0%

commit v1 on v0

--- a/solution.py
+++ b/solution.py
@@ -116,7 +116,9 @@
     images = lax.psum_scatter(
         lax.map(single, (grid_data, grid_where)), "base", scatter_dimension=0, tiled=True
     )
-    images = lax.psum(images, "freq")
+    images = images
+    for hop in (1, 2, 4):
+        images = images + lax.ppermute(images, "freq", [(dev, dev ^ hop) for dev in range(8)])
     patches = to_patch(images, subgrid_w)
     chosen, kept = slot_table(facet_owner[:, 0], base_count, FCAP)
     flattened = patches.reshape(own_subgrids, 2 * G * G)

time: 1010 us -> 970 us (0.960)
  waiting for transfers between devices: 153 us -> 117 us
    psum x1 -> x0, waiting for transfers between devices: 62.8 us -> none  [per_device(): images = lax.psum(images, 'freq')]
    ppermute x0 -> x3, waiting for transfers between devices: none -> 20 us  [per_device(): lax.ppermute(images, 'freq', [(dev, dev ^ hop) for dev in range(8)])]
  transfers between devices with their start and end apart: 4 -> 6, of which waited for: 3 -> 5; matrix products, arithmetic and copies ran while one was open for 2% -> 2% of each run, Pallas kernels for 0% -> 0%
where the time goes in v1:
time: 970 us; the launch traced here: 960 us
  other arithmetic  299 us (31%)
  local copies, waits for them, and re-layouts  220 us (23%)
  matrix products  167 us (17%)
  loops' own time  129 us (13%)
  waiting for transfers between devices  117 us (12%)
  starting transfers between devices  14.7 us (2%)
  between operations  13.7 us (1%)
    dot_general x128, matrix products, grid_one(): lax.dot_general(left, weighted, (((0,), (0,)), ((), ())), preferred_eleme...  158 us
    cos x128, other arithmetic, phase_table(): jnp.cos(outer)[:, :, None, :] * jnp.cos(inner)[:, None, :, :]  126 us
    another operation x1, loops' own time, per_device(): lax.fori_loop(0, arrived.shape[0], deposit, jnp.zeros((2, FR, GY), jnp.fl...  121 us
    dynamic_update_slice x32, local copies, waits for them, and re-layouts, deposit(): return lax.dynamic_update_slice(facet, region + patch, start)  104 us
    reduce_scatter x1, waiting for transfers between devices, per_device(): lax.psum_scatter(lax.map(single, (grid_data, grid_where)), 'base', scatte...  84.2 us
    dynamic_update_slice x128, other arithmetic, per_device(): lax.map(single, (grid_data, grid_where))  82.3 us
    slice x128, local copies, waits for them, and re-layouts, grid_one(): swapped = jnp.roll(right, G, axis=2) * signs  44.2 us
    add x32, other arithmetic, deposit(): return lax.dynamic_update_slice(facet, region + patch, start)  32 us
  transfers between devices with their start and end apart: 6, of which 5 were waited for; matrix products, arithmetic and copies ran while one was open for 2% of the time, Pallas kernels for 0%

profile of v1, /device:TPU:23, one launch (start us, length us, event | category | flops | bytes accessed | tf_op | source)
XLA Modules:
  0.0 959.5 jit_solution(12612622093094507442)
XLA Ops:
  15.9 5.3 gather_fusion.2
  21.9 490.5 %while.26 = (s32[]{:T(128)}, f32[128,2,64,64]{3,2,1,0:T(8,128)}, bf16[128,4,8]{2,1,0:T(4,128)(2,1)S(1)}, s32[]{:T(128)}, bf16[128,2,8,256]{3,2,0,1:T(8,128)(2,1)...) while((s32[]{:T(128)}, f32[128,2,64,64]{3,2,1,0:T(8,128)}, bf16[128,4,8]{2,1,0:T(4,128)(2,1)S(1)}, ...), condition=%wide.region_10.11_spmd, body=%wide.region_9.10_spmd.sunk | while | flops 71423392 | bytes 5864877 | solution.py:117
  513.5 84.2 %reduce-scatter.2.cloned.1.call-done = f32[8,2,64,64]{3,2,1,0:T(8,128)} async-done(((f32[128,2,64,64]{3,2,1,0:T(8,128)}), f32[8,2,64,64]{3,2,1,0:T(8,128)}) %reduce-scatter.2.cloned.1.call-update) | async-done | bytes 262160 | tf_op jit(solution)/shard_map/reduce_scatter | solution.py:116
  604.0 5.2 all-to-all-start
  609.3 6.8 collective-permute-done.1
  617.6 12.5 %collective-permute-done.2 = f32[8,2,64,64]{3,2,1,0:T(8,128)S(1)} collective-permute-done((f32[8,2,64,64]{3,2,1,0:T(8,128)S(1)}, f32[8,2,64,64]{3,2,1,0:T(8,128)S(1)}, u32[]{:S(2)}, u32[]{:S(2)}) %collective-permute-start.2) | collective-permute-done | bytes 262176 | tf_op jit(solution)/shard_map/ppermute | solution.py:121
  643.0 5.1 all-to-all-start.1
  648.4 12.4 %all-to-all-done.1 = f32[16,2,8192]{2,1,0:T(2,128)S(1)} async-done(((f32[16,2,8192]{2,1,0:T(2,128)}), f32[16,2,8192]{2,1,0:T(2,128)S(1)}, u32[]{:S(2)}, u32[]{:S(2)}) %all-to-all-start.1) | async-done | bytes 1048608 | tf_op jit(solution)/shard_map/all_to_all | solution.py:129
  661.5 8.1 broadcast_in_dim.170
  669.7 283.0 %while.27 = (s32[]{:T(128)}, f32[2,128,16384]{2,1,0:T(8,128)}, s32[32,2]{0,1:T(2,128)S(1)}, f32[32,8192]{1,0:T(8,128)S(1)}, s32[]{:T(128)}, /*index=5*/s32[]{:T(128)}, s32[]{:T(128)}, s32[]{:T(128)}) while((s32[]{:T(128)}, f32[2,128,16384]{2,1,0:T(8,128)}, s32[32,2]{0,1:T(2,128)S(1)}, f32[32,8192]{1,0:T(8,128)S(1)}, s32[]{:T(128)}, ...), condition=%wide.region_13.14_spmd, body=%wide.region_12.13_spmd.sunk | while | flops 8200 | bytes 295109 | solution.py:140
  675.3 3.4 dynamic_update_slice.19
  684.2 3.4 dynamic_update_slice.19
  693.2 3.4 dynamic_update_slice.19
  737.6 3.3 dynamic_update_slice.19
  746.5 3.3 dynamic_update_slice.19
  772.6 3.3 dynamic_update_slice.19
  807.0 3.4 dynamic_update_slice.19
  815.9 3.3 dynamic_update_slice.19
  824.8 3.3 dynamic_update_slice.19
  833.8 3.3 dynamic_update_slice.19
  869.3 3.3 dynamic_update_slice.19
  887.2 3.3 dynamic_update_slice.19
  904.9 3.4 dynamic_update_slice.19
  922.7 3.4 dynamic_update_slice.19
  (2281 shorter events, 630.7 us)
Async XLA Ops:
  6.5 9.4 copy-start
  6.5 15.3 %copy-start.6 = (f32[128]{0:T(128)S(1)}, f32[128]{0:T(128)}, u32[]{:S(2)}) copy-start(f32[128]{0:T(128)} %constant.174.clone.1) | copy-start | bytes 1540
  6.5 15.3 %copy-start.1 = (f32[128]{0:T(128)S(1)}, f32[128]{0:T(128)}, u32[]{:S(2)}) copy-start(f32[128]{0:T(128)} %constant.173.clone.1) | copy-start | bytes 1540
  6.5 591.1 %reduce-scatter.2.cloned.1.call-start = ((), (), s32[]{:S(2)}) async-start(), calls=%async_computation.3 | async-start | bytes 8912896 | tf_op jit(solution)/shard_map/reduce_scatter | solution.py:116
  512.3 0.7 copy-start.2
  512.3 87.7 %copy-start.3 = (s32[8]{0:T(128)S(1)}, s32[8]{0:T(128)}, u32[]{:S(2)}) copy-start(s32[8]{0:T(128)} %param.19) | copy-start | bytes 100
  512.3 87.7 %copy-start.4 = (s32[8]{0:T(128)S(1)}, s32[8]{0:T(128)}, u32[]{:S(2)}) copy-start(s32[8]{0:T(128)} %param.18) | copy-start | bytes 100
  512.3 97.0 %copy-start.5 = (f32[8]{0:T(128)S(1)}, f32[8]{0:T(128)}, u32[]{:S(2)}) copy-start(f32[8]{0:T(128)} %param.16) | copy-start | bytes 100
  597.7 4.1 collective-permute-start
  602.9 13.2 %collective-permute-start.1 = (f32[8,2,64,64]{3,2,1,0:T(8,128)S(1)}, f32[8,2,64,64]{3,2,1,0:T(8,128)S(1)}, u32[]{:S(2)}, u32[]{:S(2)}) collective-permute-start(f32[8,2,64,64]{3,2,1,0:T(8,128)S(1)} %add.333), channel_id=1, source_target_pairs={{0,2},{1,3},{2,0},{3,1},{4,6},{5,7},{6,4},{7,5},{8,10},{9,11},{10,... | collective-permute-start | bytes 786440 | tf_op jit(solution)/shard_map/ppermute | solution.py:121
  604.0 39.0 %all-to-all-start = ((f32[16,2,2]{1,2,0:T(2,128)}), f32[16,2,2]{1,2,0:T(2,128)S(1)}, u32[]{:S(2)}, u32[]{:S(2)}) async-start(f32[16,2,2]{1,2,0:T(2,128)} %copy.84), calls=%async_computation | async-start | bytes 32768 | tf_op jit(solution)/shard_map/all_to_all | solution.py:130
  616.2 14.0 %collective-permute-start.2 = (f32[8,2,64,64]{3,2,1,0:T(8,128)S(1)}, f32[8,2,64,64]{3,2,1,0:T(8,128)S(1)}, u32[]{:S(2)}, u32[]{:S(2)}) collective-permute-start(f32[8,2,64,64]{3,2,1,0:T(8,128)S(1)} %add.334), channel_id=1, source_target_pairs={{0,4},{1,5},{2,6},{3,7},{4,0},{5,1},{6,2},{7,3},{8,12},{9,13},{10,... | collective-permute-start | bytes 786440 | tf_op jit(solution)/shard_map/ppermute | solution.py:121
  643.0 17.8 %all-to-all-start.1 = ((f32[16,2,8192]{2,1,0:T(2,128)}), f32[16,2,8192]{2,1,0:T(2,128)S(1)}, u32[]{:S(2)}, u32[]{:S(2)}) async-start(f32[16,2,8192]{2,1,0:T(2,128)} %select_select_fusion), calls=%async_computation.2 | async-start | bytes 2097152 | tf_op jit(solution)/shard_map/all_to_all | solution.py:129
Sparse Core Ops, SparseCore 0:
  512.5 85.1 reduce-scatter.1
